TPU v7x, 32 devices: a whole 2x2x4 slice. The times are simulated.
32 devices in a mesh: seq: 8 (over y, x, core), tensor: 4 (over z).
Axes of the slice: x: 2, y: 2, z: 4, core: 2. Of those that a mesh axis runs over, the one named last changes fastest.
Arguments:
- queries: bfloat16 [1024, 4096], P('seq', 'tensor'), may hold values from -6 to 6
- keyvals: bfloat16 [16, 64, 1024], P('seq', 'tensor'), may hold values from -6 to 6
- reader_images: int32 [8, 3], replicated, may hold values from 0 to 15, as said below
- read_spans: int32 [2, 1024], P(None, 'seq'), may hold values from 0 to 3, as said below
- query_gain: float32 [128], replicated, may hold values from 1 to 2
- key_gain: float32 [128], replicated, may hold values from 1 to 2
- out_grad: bfloat16 [1024, 4096], P('seq', 'tensor'), may hold values from -6 to 6
Outputs:
- attention: bfloat16 [1024, 4096], P('seq', 'tensor')
- query_grad: bfloat16 [1024, 4096], P('seq', 'tensor')
- keyval_grad: bfloat16 [16, 64, 1024], P('seq', 'tensor')
Inputs may be any that keep to these rules, and one draw needn't show every extreme that they name: `reader_images`: slot r of row j names an image held by text shard (j - r) modulo 8, that is one of images ((j - r) mod 8) * 2 to ((j - r) mod 8) * 2 + 1. A text token reads slots read_spans[0] to read_spans[1] - 1 of its shard's row of reader_images; one that reads none has 0 and 0; text shard j reads no slot r > j; some shard reads all 3 slots.
All inputs are finite; a program needn't handle non-finite values.
Results may differ from a plain program's by a relative error of at most 0.0095.
Values may be sent and summed in bfloat16 or wider, within the bound.
A program may use at most 64 MiB of HBM per device.

v0:
```python
import jax
import jax.numpy as jnp
from jax import lax
from jax.sharding import PartitionSpec as P

EPSILON = 1e-05


def shifted(array, axis, by):
    length = lax.axis_size(axis)
    pairs = [(i, i + by) for i in range(length) if 0 <= i + by < length]
    return lax.ppermute(array, axis, pairs)


def shortened(array):

    def short(part):
        return part.astype(jnp.bfloat16) if part.dtype == jnp.float32 else part

    return jax.tree.map(short, array)


def norm_scale(values, weights):
    inverse = lax.rsqrt(jnp.mean(values * values, axis=-1, keepdims=True) + EPSILON)
    return values * inverse * weights


def norm_back(values, weights, upstream):
    inverse = lax.rsqrt(jnp.mean(values * values, axis=-1, keepdims=True) + EPSILON)
    scaled = weights * upstream
    return inverse * scaled - values * inverse * inverse * inverse * jnp.mean(
        values * scaled, axis=-1, keepdims=True
    )


def local(queries, keyvals, reader_images, read_spans, query_gain, key_gain, out_grad):
    seq_count = lax.axis_size("seq")
    tensor_count = lax.axis_size("tensor")
    my_shard = lax.axis_index("seq")
    image_count = keyvals.shape[0]
    sub_rows = keyvals.shape[1]
    head_width = query_gain.shape[0]
    score_scale = head_width ** (-0.5)
    token_count = queries.shape[0]
    group_size = queries.shape[1] // head_width
    piece_rows = tensor_count * sub_rows
    slot_total = reader_images.shape[1]
    slot_ids = jnp.arange(slot_total, dtype=jnp.int32)
    reader_rows = jnp.minimum(my_shard + slot_ids, seq_count - 1)
    picks = reader_images[reader_rows, slot_ids] - my_shard * image_count
    picks = jnp.clip(picks, 0, image_count - 1)
    holder_rows = keyvals.reshape(image_count, sub_rows, tensor_count, 2 * head_width)
    own_head = lax.all_to_all(holder_rows, "tensor", split_axis=2, concat_axis=1, tiled=True)
    own_head = own_head.reshape(image_count, piece_rows, 2 * head_width)
    chosen = jnp.take(own_head, picks, axis=0)
    pieces = [chosen[0]]
    for slot_number in range(1, slot_total):
        pieces.append(shifted(chosen[slot_number], "seq", slot_number))
    arrived = jnp.stack(pieces, axis=0)
    slot_keys_raw = arrived[..., :head_width]
    slot_values = arrived[..., head_width:]
    slot_hat = norm_scale(slot_keys_raw.astype(jnp.float32), key_gain).astype(jnp.bfloat16)
    query_float = queries.reshape(token_count, group_size, head_width).astype(jnp.float32)
    query_hat = norm_scale(query_float, query_gain).astype(jnp.bfloat16)
    slot_masks = (
        (read_spans[0][None, :] <= slot_ids[:, None]) & (slot_ids[:, None] < read_spans[1][None, :])
    ).astype(jnp.float32)
    no_image = 1.0 - jnp.max(slot_masks, axis=0)
    denominator = jnp.broadcast_to(no_image[:, None], (token_count, group_size))
    numerator = jnp.zeros((token_count, group_size, head_width), jnp.float32)
    weight_list = []
    for slot_number in range(slot_total):
        scores = (
            jnp.einsum(
                "tad,ud->tau", query_hat, slot_hat[slot_number], preferred_element_type=jnp.float32
            )
            * score_scale
        )
        weights = jnp.exp(scores) * slot_masks[slot_number][:, None, None]
        denominator = denominator + jnp.sum(weights, axis=-1)
        numerator = numerator + jnp.einsum(
            "tau,ud->tad",
            weights.astype(jnp.bfloat16),
            slot_values[slot_number],
            preferred_element_type=jnp.float32,
        )
        weight_list.append(weights)
    attended = (numerator / denominator[..., None]).astype(jnp.bfloat16)
    grad_out = out_grad.reshape(token_count, group_size, head_width)
    dot_rows = jnp.sum(grad_out.astype(jnp.float32) * attended.astype(jnp.float32), axis=-1)
    grad_query_hat = jnp.zeros((token_count, group_size, head_width), jnp.float32)
    slot_grads = []
    for slot_number in range(slot_total):
        probabilities = weight_list[slot_number] / denominator[..., None]
        grad_probs = jnp.einsum(
            "tad,ud->tau", grad_out, slot_values[slot_number], preferred_element_type=jnp.float32
        )
        grad_scores = (probabilities * (grad_probs - dot_rows[..., None])).astype(jnp.bfloat16)
        grad_query_hat = (
            grad_query_hat
            + jnp.einsum(
                "tau,ud->tad",
                grad_scores,
                slot_hat[slot_number],
                preferred_element_type=jnp.float32,
            )
            * score_scale
        )
        grad_key = (
            jnp.einsum("tau,tad->ud", grad_scores, query_hat, preferred_element_type=jnp.float32)
            * score_scale
        )
        grad_value = jnp.einsum(
            "tau,tad->ud",
            probabilities.astype(jnp.bfloat16),
            grad_out,
            preferred_element_type=jnp.float32,
        )
        grad_key = norm_back(slot_keys_raw[slot_number].astype(jnp.float32), key_gain, grad_key)
        slot_grads.append(jnp.concatenate([grad_key, grad_value], axis=-1))
    grad_query = norm_back(query_float, query_gain, grad_query_hat).astype(jnp.bfloat16)
    grad_query = grad_query.reshape(token_count, group_size * head_width)
    returning = jnp.stack(slot_grads, axis=0)
    valid_reader = my_shard + slot_ids < seq_count
    selector = (
        (picks[None, :] == jnp.arange(image_count, dtype=jnp.int32)[:, None])
        & valid_reader[None, :]
    ).astype(jnp.float32)
    backs = [returning[0]]
    for slot_number in range(1, slot_total):
        backs.append(
            shifted(returning[slot_number].astype(jnp.bfloat16), "seq", -slot_number).astype(
                jnp.float32
            )
        )
    at_holder = jnp.stack(backs, axis=0)
    summed = jnp.dot(selector, at_holder.reshape(slot_total, -1), precision=lax.Precision.HIGHEST)
    summed = summed.reshape(image_count, piece_rows, 1, 2 * head_width)
    holder_grads = lax.all_to_all(
        shortened(summed), "tensor", split_axis=1, concat_axis=2, tiled=True
    ).astype(summed.dtype)
    grad_key_part = holder_grads[..., :head_width]
    keyval_grad = jnp.concatenate([grad_key_part, holder_grads[..., head_width:]], axis=-1).astype(
        jnp.bfloat16
    )
    keyval_grad = keyval_grad.reshape(image_count, sub_rows, tensor_count * 2 * head_width)
    return (attended.reshape(token_count, group_size * head_width), grad_query, keyval_grad)


def solution(mesh):
    placed = (
        P("seq", "tensor"),
        P("seq", "tensor", None),
        P(),
        P(None, "seq"),
        P(),
        P(),
        P("seq", "tensor"),
    )
    return jax.shard_map(
        local,
        mesh=mesh,
        in_specs=placed,
        out_specs=(P("seq", "tensor"), P("seq", "tensor"), P("seq", "tensor", None)),
        check_vma=False,
    )
```

profile of v0, /device:TPU:0, one launch (start us, length us, event | category | flops | bytes accessed | tf_op | source)
XLA Modules:
  0.0 47.3 jit_solution(9747753883789277437)
XLA Ops:
  0.6 1.5 %copy.119 = bf16[2,2,4,8,256]{4,3,1,0,2:T(8,128)(2,1)} copy(bf16[2,2,4,8,256]{4,3,2,1,0:T(8,128)(2,1)} %bitcast.235) | data formatting | bytes 131072 | tf_op jit(solution)/shard_map/reshape | solution.py:52
  2.1 6.3 %all-to-all-start = ((bf16[2,16,4,256]{3,1,0,2:T(8,128)(2,1)}), bf16[2,16,4,256]{3,1,0,2:T(8,128)(2,1)S(1)}, u32[]{:S(2)}, u32[]{:S(2)}) async-start(bf16[2,16,4,256]{3,1,0,2:T(8,128)(2,1)} %bitcast.207), calls=%async_computation | async-start | bytes 131072 | tf_op jit(solution)/shard_map/all_to_all | solution.py:53
  8.5 0.7 %copy-done.4 = s32[2,128]{1,0:T(2,128)S(1)} copy-done((s32[2,128]{1,0:T(2,128)S(1)}, s32[2,128]{1,0:T(2,128)}, u32[]{:S(2)}) %copy-start.4) | copy-done | bytes 1048
  9.2 0.6 %copy-done.3 = f32[128]{0:T(128)S(1)} copy-done((f32[128]{0:T(128)S(1)}, f32[128]{0:T(128)}, u32[]{:S(2)}) %copy-start.3) | copy-done | bytes 536
  9.9 0.6 %copy-done.5 = f32[128]{0:T(128)S(1)} copy-done((f32[128]{0:T(128)S(1)}, f32[128]{0:T(128)}, u32[]{:S(2)}) %copy-start.5) | copy-done | bytes 536
  10.5 0.7 %gather_fusion = s32[3]{0:T(128)S(1)} fusion(s32[8,3]{0,1:T(4,128)S(1)} %copy-done, s32[3]{0:T(128)S(1)} %fusion.74), kind=kCustom, calls=%fused_computation | custom fusion | bytes 48 | tf_op jit(solution)/shard_map/gather | solution.py:50
  12.0 2.2 %all-to-all-done = bf16[2,16,4,256]{3,1,0,2:T(8,128)(2,1)S(1)} async-done(((bf16[2,16,4,256]{3,1,0,2:T(8,128)(2,1)}), bf16[2,16,4,256]{3,1,0,2:T(8,128)(2,1)S(1)}, u32[]{:S(2)}, u32[]{:S(2)}) %all-to-all-start) | async-done | bytes 65568 | tf_op jit(solution)/shard_map/all_to_all | solution.py:53
  14.2 0.6 %gather_fusion.1 = bf16[3,64,256]{2,1,0:T(8,128)(2,1)S(1)} fusion(bf16[2,64,256]{2,1,0:T(8,128)(2,1)S(1)} %bitcast.211, s32[1024]{0:T(1024)S(1)} %pad_clamp_fusion), kind=kCustom, calls=%fused_computation.1 | custom fusion | bytes 196620 | tf_op jit(solution)/shard_map/jit(_take)/gather | solution.py:55
  14.9 3.4 %collective-permute-start.1 = (bf16[64,256]{1,0:T(8,128)(2,1)S(1)}, bf16[64,256]{1,0:T(8,128)(2,1)S(1)}, u32[]{:S(2)}, u32[]{:S(2)}) collective-permute-start(bf16[64,256]{1,0:T(8,128)(2,1)S(1)} %get-tuple-element.26), channel_id=1, source_target_pairs={{0,8},{4,12},{8,16},{12,20},{16,24},{20,28},{1,9},{5,13},{9,17},{1... | collective-permute-start | bytes 98312 | tf_op jit(solution)/shard_map/ppermute | solution.py:12
  18.3 1.3 %collective-permute-start = (bf16[64,256]{1,0:T(8,128)(2,1)S(1)}, bf16[64,256]{1,0:T(8,128)(2,1)S(1)}, u32[]{:S(2)}, u32[]{:S(2)}) collective-permute-start(bf16[64,256]{1,0:T(8,128)(2,1)S(1)} %get-tuple-element.27), channel_id=1, source_target_pairs={{0,4},{4,8},{8,12},{12,16},{16,20},{20,24},{24,28},{1,5},{5,9},{9,... | collective-permute-start | bytes 98312 | tf_op jit(solution)/shard_map/ppermute | solution.py:12
  19.9 0.6 %collective-permute-done = bf16[64,256]{1,0:T(8,128)(2,1)S(1)} collective-permute-done((bf16[64,256]{1,0:T(8,128)(2,1)S(1)}, bf16[64,256]{1,0:T(8,128)(2,1)S(1)}, u32[]{:S(2)}, u32[]{:S(2)}) %collective-permute-start) | collective-permute-done | bytes 32800 | tf_op jit(solution)/shard_map/ppermute | solution.py:12
  22.5 0.3 multiply_reduce_fusion.1
  24.8 0.3 fusion.47
  25.1 0.3 fusion.41
  25.5 1.3 %collective-permute-start.2 = (bf16[64,256]{1,0:T(8,128)(2,1)S(1)}, bf16[64,256]{1,0:T(8,128)(2,1)S(1)}, u32[]{:S(2)}, u32[]{:S(2)}) collective-permute-start(bf16[64,256]{1,0:T(8,128)(2,1)S(1)} %pad_maximum_fusion.3), channel_id=1, source_target_pairs={{4,0},{8,4},{12,8},{16,12},{20,16},{24,20},{28,24},{5,1},{9,5},{13... | collective-permute-start | bytes 98312 | tf_op jit(solution)/shard_map/ppermute | solution.py:12
  27.1 1.3 %collective-permute-start.3 = (bf16[64,256]{1,0:T(8,128)(2,1)S(1)}, bf16[64,256]{1,0:T(8,128)(2,1)S(1)}, u32[]{:S(2)}, u32[]{:S(2)}) collective-permute-start(bf16[64,256]{1,0:T(8,128)(2,1)S(1)} %pad_maximum_fusion.4), channel_id=1, source_target_pairs={{8,0},{12,4},{16,8},{20,12},{24,16},{28,20},{9,1},{13,5},{17,9},{2... | collective-permute-start | bytes 98312 | tf_op jit(solution)/shard_map/ppermute | solution.py:12
  28.4 2.1 %collective-permute-done.2 = bf16[64,256]{1,0:T(8,128)(2,1)S(1)} collective-permute-done((bf16[64,256]{1,0:T(8,128)(2,1)S(1)}, bf16[64,256]{1,0:T(8,128)(2,1)S(1)}, u32[]{:S(2)}, u32[]{:S(2)}) %collective-permute-start.2) | collective-permute-done | bytes 32800 | tf_op jit(solution)/shard_map/ppermute | solution.py:12
  30.6 5.7 %collective-permute-done.3 = bf16[64,256]{1,0:T(8,128)(2,1)S(1)} collective-permute-done((bf16[64,256]{1,0:T(8,128)(2,1)S(1)}, bf16[64,256]{1,0:T(8,128)(2,1)S(1)}, u32[]{:S(2)}, u32[]{:S(2)}) %collective-permute-start.3) | collective-permute-done | bytes 32800 | tf_op jit(solution)/shard_map/ppermute | solution.py:12
  36.6 1.0 %fusion.18 = bf16[2,64,1,256]{3,0,2,1:T(2,128)(2,1)} fusion(f32[64,256,3]{1,2,0:T(4,128)S(1)} %bitcast.209, pred[3]{0:T(512)(128)(4,1)S(1)} %add_compare_fusion, s32[3]{0:T(128)S(1)} %get-tuple-element.22), kind=kOutput, calls=%fused_computation.31 | convolution fusion | flops 1212428 | bytes 262159 | tf_op jit(solution)/shard_map/dot_general | solution.py:137
  37.6 3.3 %all-to-all-start.1 = ((bf16[2,64,1,256]{3,0,2,1:T(2,128)(2,1)}), bf16[2,64,1,256]{3,0,2,1:T(2,128)(2,1)S(1)}, u32[]{:S(2)}, u32[]{:S(2)}) async-start(bf16[2,64,1,256]{3,0,2,1:T(2,128)(2,1)} %fusion.18), calls=%async_computation.1 | async-start | bytes 131072 | tf_op jit(solution)/shard_map/all_to_all | solution.py:139
  40.9 0.9 %copy.84 = bf16[128,1024]{1,0:T(8,128)(2,1)} copy(bf16[128,1024]{0,1:T(8,128)(2,1)S(1)} %bitcast.227) | data formatting | bytes 524288
  41.7 0.8 %copy.85 = bf16[128,1024]{1,0:T(8,128)(2,1)} copy(bf16[128,1024]{0,1:T(8,128)(2,1)S(1)} %bitcast.210) | data formatting | bytes 524288
  42.6 4.0 %all-to-all-done.1 = bf16[2,64,1,256]{3,0,2,1:T(2,128)(2,1)S(1)} async-done(((bf16[2,64,1,256]{3,0,2,1:T(2,128)(2,1)}), bf16[2,64,1,256]{3,0,2,1:T(2,128)(2,1)S(1)}, u32[]{:S(2)}, u32[]{:S(2)}) %all-to-all-start.1) | async-done | bytes 65568 | tf_op jit(solution)/shard_map/all_to_all | solution.py:139
  46.6 0.7 %reshape.208 = bf16[2,16,1024]{2,1,0:T(8,128)(2,1)} reshape(bf16[2,16,4,1,256]{4,2,1,0,3:T(4,128)(2,1)S(1)} %copy.83) | data formatting | bytes 131072 | tf_op jit(solution)/shard_map/reshape | solution.py:146
  (70 shorter events, 5.8 us)
Async XLA Ops:
  0.6 9.9 %copy-start = (s32[8,3]{0,1:T(4,128)S(1)}, s32[8,3]{0,1:T(4,128)}, u32[]{:S(2)}) copy-start(s32[8,3]{0,1:T(4,128)} %param.9) | copy-start | bytes 292
  2.1 12.1 %all-to-all-start = ((bf16[2,16,4,256]{3,1,0,2:T(8,128)(2,1)}), bf16[2,16,4,256]{3,1,0,2:T(8,128)(2,1)S(1)}, u32[]{:S(2)}, u32[]{:S(2)}) async-start(bf16[2,16,4,256]{3,1,0,2:T(8,128)(2,1)} %bitcast.207), calls=%async_computation | async-start | bytes 131072 | tf_op jit(solution)/shard_map/all_to_all | solution.py:53
  8.5 0.7 %copy-start.4 = (s32[2,128]{1,0:T(2,128)S(1)}, s32[2,128]{1,0:T(2,128)}, u32[]{:S(2)}) copy-start(s32[2,128]{1,0:T(2,128)} %param.10) | copy-start | bytes 3076
  9.2 0.7 %copy-start.3 = (f32[128]{0:T(128)S(1)}, f32[128]{0:T(128)}, u32[]{:S(2)}) copy-start(f32[128]{0:T(128)} %param.11) | copy-start | bytes 1540
  9.8 0.7 %copy-start.5 = (f32[128]{0:T(128)S(1)}, f32[128]{0:T(128)}, u32[]{:S(2)}) copy-start(f32[128]{0:T(128)} %param.12) | copy-start | bytes 1540
  10.5 1.0 %copy-start.1 = (bf16[128,1024]{1,0:T(8,128)(2,1)S(1)}, bf16[128,1024]{1,0:T(8,128)(2,1)}, u32[]{:S(2)}) copy-start(bf16[128,1024]{1,0:T(8,128)(2,1)} %param.7) | copy-start | bytes 786436
  14.2 5.4 %copy-start.2 = (bf16[128,1024]{1,0:T(8,128)(2,1)S(1)}, bf16[128,1024]{1,0:T(8,128)(2,1)}, u32[]{:S(2)}) copy-start(bf16[128,1024]{1,0:T(8,128)(2,1)} %param.13) | copy-start | bytes 786436
  14.9 5.0 %collective-permute-start.1 = (bf16[64,256]{1,0:T(8,128)(2,1)S(1)}, bf16[64,256]{1,0:T(8,128)(2,1)S(1)}, u32[]{:S(2)}, u32[]{:S(2)}) collective-permute-start(bf16[64,256]{1,0:T(8,128)(2,1)S(1)} %get-tuple-element.26), channel_id=1, source_target_pairs={{0,8},{4,12},{8,16},{12,20},{16,24},{20,28},{1,9},{5,13},{9,17},{1... | collective-permute-start | bytes 98312 | tf_op jit(solution)/shard_map/ppermute | solution.py:12
  18.3 2.1 %collective-permute-start = (bf16[64,256]{1,0:T(8,128)(2,1)S(1)}, bf16[64,256]{1,0:T(8,128)(2,1)S(1)}, u32[]{:S(2)}, u32[]{:S(2)}) collective-permute-start(bf16[64,256]{1,0:T(8,128)(2,1)S(1)} %get-tuple-element.27), channel_id=1, source_target_pairs={{0,4},{4,8},{8,12},{12,16},{16,20},{20,24},{24,28},{1,5},{5,9},{9,... | collective-permute-start | bytes 98312 | tf_op jit(solution)/shard_map/ppermute | solution.py:12
  25.5 5.0 %collective-permute-start.2 = (bf16[64,256]{1,0:T(8,128)(2,1)S(1)}, bf16[64,256]{1,0:T(8,128)(2,1)S(1)}, u32[]{:S(2)}, u32[]{:S(2)}) collective-permute-start(bf16[64,256]{1,0:T(8,128)(2,1)S(1)} %pad_maximum_fusion.3), channel_id=1, source_target_pairs={{4,0},{8,4},{12,8},{16,12},{20,16},{24,20},{28,24},{5,1},{9,5},{13... | collective-permute-start | bytes 98312 | tf_op jit(solution)/shard_map/ppermute | solution.py:12
  27.1 9.2 %collective-permute-start.3 = (bf16[64,256]{1,0:T(8,128)(2,1)S(1)}, bf16[64,256]{1,0:T(8,128)(2,1)S(1)}, u32[]{:S(2)}, u32[]{:S(2)}) collective-permute-start(bf16[64,256]{1,0:T(8,128)(2,1)S(1)} %pad_maximum_fusion.4), channel_id=1, source_target_pairs={{8,0},{12,4},{16,8},{20,12},{24,16},{28,20},{9,1},{13,5},{17,9},{2... | collective-permute-start | bytes 98312 | tf_op jit(solution)/shard_map/ppermute | solution.py:12
  37.6 9.0 %all-to-all-start.1 = ((bf16[2,64,1,256]{3,0,2,1:T(2,128)(2,1)}), bf16[2,64,1,256]{3,0,2,1:T(2,128)(2,1)S(1)}, u32[]{:S(2)}, u32[]{:S(2)}) async-start(bf16[2,64,1,256]{3,0,2,1:T(2,128)(2,1)} %fusion.18), calls=%async_computation.1 | async-start | bytes 131072 | tf_op jit(solution)/shard_map/all_to_all | solution.py:139
where the time goes:
time: 47.8 us; the launch traced here: 47.3 us
  starting transfers between devices  16.9 us (35%)
  waiting for transfers between devices  14.6 us (31%)
  local copies, waits for them, and re-layouts  8.1 us (17%)
  matrix products  5.42 us (11%)
  other arithmetic  1.18 us (2%)
  between operations  1.07 us (2%)
    ppermute x4, waiting for transfers between devices, shifted(): return lax.ppermute(array, axis, pairs)  8.43 us
    ppermute x4, starting transfers between devices, shifted(): return lax.ppermute(array, axis, pairs)  7.27 us
    all_to_all x1, starting transfers between devices, local(): lax.all_to_all(holder_rows, 'tensor', split_axis=2, concat_axis=1, tiled=...  6.35 us
    unnamed x18, local copies, waits for them, and re-layouts  4.31 us
    all_to_all x1, waiting for transfers between devices, local(): lax.all_to_all(shortened(summed), 'tensor', split_axis=1, concat_axis=2,...  4.01 us
    all_to_all x1, starting transfers between devices, local(): lax.all_to_all(shortened(summed), 'tensor', split_axis=1, concat_axis=2,...  3.28 us
    all_to_all x1, waiting for transfers between devices, local(): lax.all_to_all(holder_rows, 'tensor', split_axis=2, concat_axis=1, tiled=...  2.2 us
    reshape x1, local copies, waits for them, and re-layouts, local(): keyvals.reshape(image_count, sub_rows, tensor_count, 2 * head_width)  1.48 us
  transfers between devices with their start and end apart: 6, of which 6 were waited for; matrix products, arithmetic and copies ran while one was open for 7% of the time, Pallas kernels for 0%

commit v1 on v0

v1 whole, which is shorter than its diff:
```python
import functools

import jax
import jax.numpy as jnp
from jax import lax
from jax.experimental import pallas as pl
from jax.experimental.pallas import tpu as pltpu
from jax.sharding import PartitionSpec as P

EPSILON = 1e-05
MESH = pl.DeviceIdType.MESH
F32 = jnp.float32
BF16 = jnp.bfloat16
ROWS = (((1,), (1,)), ((), ()))
COLUMNS = (((0,), (0,)), ((), ()))


def inverse_of(values):
    return lax.rsqrt(jnp.mean(values * values, axis=-1, keepdims=True) + EPSILON)


def dot(a, b, dims=None):
    if dims is None:
        return jnp.dot(a, b, preferred_element_type=F32)
    return lax.dot_general(a, b, dims, preferred_element_type=F32)


def kernel(
    seq_count, tensor_count,
    images_ref, spans_ref, query_gain_ref, key_gain_ref, kv_hbm, q_hbm, do_hbm,
    att_hbm, qg_hbm, kvg_hbm,
    kv, q, do, qhat, send, arrive, gsend, garrive, wb, dsb, att, qg, kvg, denoms,
    in_sem, out_sem, send_sem, recv_sem, gsend_sem, grecv_sem,
):
    s = lax.axis_index("seq")
    t = lax.axis_index("tensor")
    slots, _, sub, width2 = arrive.shape
    width = width2 // 2
    image_count = kv.shape[0]
    tokens = q.shape[0]
    group = q.shape[1] // width
    image_rows = tensor_count * sub
    all_rows = slots * image_rows
    scale = width ** (-0.5)

    def ring(k):
        return lax.rem(t + k, tensor_count)

    kv_in = pltpu.make_async_copy(kv_hbm, kv, in_sem.at[0])
    q_in = pltpu.make_async_copy(q_hbm, q, in_sem.at[1])
    do_in = pltpu.make_async_copy(do_hbm, do, in_sem.at[2])
    kv_in.start()
    q_in.start()
    do_in.start()

    barrier = pltpu.get_barrier_semaphore()
    for shift in range(1 - slots, slots):

        def greet(shift=shift):
            for k in range(tensor_count):
                if shift or k:
                    pl.semaphore_signal(
                        barrier, inc=1, device_id=(s + shift, ring(k)), device_id_type=MESH
                    )

        if shift == 0:
            greet()
        else:
            pl.when((s + shift >= 0) & (s + shift < seq_count))(greet)

    picks = []
    for r in range(slots):
        reader = jnp.minimum(s + r, seq_count - 1)
        pick = images_ref[reader, r] - s * image_count
        picks.append(jnp.clip(pick, 0, image_count - 1))

    kv_in.wait()
    for r in range(slots):
        chosen = kv[picks[r]]
        for k in range(tensor_count):
            send[r, k] = chosen[:, k * width2 : (k + 1) * width2]
    arrive[0, t] = send[0, t]
    for r in range(1, slots):

        @pl.when(s < r)
        def _(r=r):
            arrive[r] = jnp.zeros(arrive.shape[1:], BF16)

        @pl.when(s + r >= seq_count)
        def _(r=r):
            garrive[r] = jnp.zeros(garrive.shape[1:], BF16)

    near = jnp.minimum(s, slots - 1) + jnp.minimum(seq_count - 1 - s, slots - 1) + 1
    pl.semaphore_wait(barrier, near * tensor_count - 1)

    def forward(r, k, slot):
        return pltpu.make_async_remote_copy(
            src_ref=send.at[r, ring(k)], dst_ref=arrive.at[r, slot],
            send_sem=send_sem.at[r, k], recv_sem=recv_sem.at[r, k],
            device_id=(s + r, ring(k)), device_id_type=MESH,
        )

    def backward(r, k, slot):
        return pltpu.make_async_remote_copy(
            src_ref=gsend.at[r, ring(k)], dst_ref=garrive.at[r, slot],
            send_sem=gsend_sem.at[r, k], recv_sem=grecv_sem.at[r, k],
            device_id=(s - r, ring(k)), device_id_type=MESH,
        )

    def each(r, condition, body):
        def run():
            for k in reversed(range(tensor_count)):
                if r or k:
                    body(k)

        if r == 0:
            run()
        else:
            pl.when(condition)(run)

    def from_ring(k):
        return lax.rem(t + tensor_count - k, tensor_count)

    for r in reversed(range(slots)):
        each(r, s + r < seq_count, lambda k, r=r: forward(r, k, t).start())

    query_gain = query_gain_ref[...]
    key_gain = key_gain_ref[...]
    q_in.wait()
    for a in range(group):
        qf = q[:, a * width : (a + 1) * width].astype(F32)
        qhat[a] = (qf * inverse_of(qf) * query_gain).astype(BF16)
    do_in.wait()

    begins = spans_ref[0:1, :]
    ends = spans_ref[1:2, :]
    masks = [((begins <= r) & (r < ends)).astype(F32) for r in range(slots)]
    no_image = 1.0 - functools.reduce(jnp.maximum, masks)
    mask = jnp.concatenate(
        [jnp.broadcast_to(m, (image_rows, tokens)) for m in masks], axis=0
    )

    for r in range(slots):
        each(r, s >= r, lambda k, r=r: forward(r, k, from_ring(k)).wait_recv())

    arrived = arrive[...].reshape(all_rows, width2)
    keys = arrived[:, :width].astype(F32)
    values = arrived[:, width:]
    key_hat = (keys * inverse_of(keys) * key_gain).astype(BF16)

    grad_key = jnp.zeros((all_rows, width), F32)
    grad_value = jnp.zeros((all_rows, width), F32)
    for a in range(group):
        grad_out = do[:, a * width : (a + 1) * width]
        query = qhat[a]
        weights = jnp.exp(dot(key_hat, query, ROWS) * scale) * mask
        denominator = jnp.sum(weights, axis=0, keepdims=True) + no_image
        probs = weights * (1.0 / denominator)
        grad_probs = dot(values, grad_out, ROWS)
        row_dot = jnp.sum(probs * grad_probs, axis=0, keepdims=True)
        score_grad = (probs * (grad_probs - row_dot)).astype(BF16)
        wb[a] = weights.astype(BF16)
        dsb[a] = score_grad
        denoms[a : a + 1, :] = denominator
        grad_key = grad_key + dot(score_grad, query)
        grad_value = grad_value + dot(probs.astype(BF16), grad_out)
    piece = (slots, tensor_count, sub, width)
    gsend[:, :, :, :width] = (grad_key * scale).astype(BF16).reshape(piece)
    gsend[:, :, :, width:] = grad_value.astype(BF16).reshape(piece)

    for r in reversed(range(slots)):
        each(r, s >= r, lambda k, r=r: backward(r, k, t).start())
    garrive[0, t] = gsend[0, t]

    padded = jnp.concatenate(
        [denoms[...], jnp.ones((tokens - group, tokens), F32)], axis=0
    ) if tokens > group else denoms[...]
    columns = 1.0 / jnp.transpose(padded)
    for a in range(group):
        part = slice(a * width, (a + 1) * width)
        numerator = dot(wb[a], values, COLUMNS)
        att[:, part] = (numerator * columns[:, a : a + 1]).astype(BF16)
    att_out = pltpu.make_async_copy(att, att_hbm, out_sem.at[0])
    att_out.start()
    for a in range(group):
        part = slice(a * width, (a + 1) * width)
        scaled = query_gain * (dot(dsb[a], key_hat, COLUMNS) * scale)
        qf = q[:, part].astype(F32)
        inverse = inverse_of(qf)
        mean = jnp.mean(qf * scaled, axis=-1, keepdims=True)
        qg[:, part] = (inverse * scaled - qf * (inverse * inverse * inverse * mean)).astype(BF16)
    qg_out = pltpu.make_async_copy(qg, qg_hbm, out_sem.at[1])
    qg_out.start()

    for r in range(slots):
        each(r, s + r < seq_count, lambda k, r=r: backward(r, k, from_ring(k)).wait_recv())

    for i in range(image_count):
        chosen = [(picks[r] == i) & (s + r < seq_count) for r in range(slots)]
        for h in range(tensor_count):
            total = jnp.zeros((sub, width2), F32)
            for r in range(slots):
                total = total + jnp.where(chosen[r], garrive[r, h].astype(F32), 0.0)
            start = h * width2
            raw = kv[i, :, start : start + width].astype(F32)
            inverse = inverse_of(raw)
            scaled = key_gain * total[:, :width]
            mean = jnp.mean(raw * scaled, axis=-1, keepdims=True)
            kvg[i, :, start : start + width] = (
                inverse * scaled - raw * (inverse * inverse * inverse * mean)
            ).astype(BF16)
            kvg[i, :, start + width : start + width2] = total[:, width:].astype(BF16)
    kvg_out = pltpu.make_async_copy(kvg, kvg_hbm, out_sem.at[2])
    kvg_out.start()

    for r in range(slots):
        each(r, s + r < seq_count, lambda k, r=r: forward(r, k, t).wait_send())
        each(r, s >= r, lambda k, r=r: backward(r, k, t).wait_send())
    att_out.wait()
    qg_out.wait()
    kvg_out.wait()


def local(seq_count, tensor_count, queries, keyvals, reader_images, read_spans, query_gain, key_gain, out_grad):
    width = query_gain.shape[0]
    tokens, columns = queries.shape
    group = columns // width
    image_count, sub, _ = keyvals.shape
    slots = reader_images.shape[1]
    rows = slots * tensor_count * sub
    pieces = (slots, tensor_count, sub, 2 * width)
    whole = pl.BlockSpec(memory_space=pltpu.VMEM)
    placed = pl.BlockSpec(memory_space=pl.ANY)
    pairs = (slots, tensor_count)
    return pl.pallas_call(
        functools.partial(kernel, seq_count, tensor_count),
        out_shape=(
            jax.ShapeDtypeStruct(queries.shape, BF16),
            jax.ShapeDtypeStruct(queries.shape, BF16),
            jax.ShapeDtypeStruct(keyvals.shape, BF16),
        ),
        in_specs=[pl.BlockSpec(memory_space=pltpu.SMEM), whole, whole, whole, placed, placed, placed],
        out_specs=(placed, placed, placed),
        scratch_shapes=[
            pltpu.VMEM(keyvals.shape, BF16),
            pltpu.VMEM(queries.shape, BF16),
            pltpu.VMEM(queries.shape, BF16),
            pltpu.VMEM((group, tokens, width), BF16),
            pltpu.VMEM(pieces, BF16),
            pltpu.VMEM(pieces, BF16),
            pltpu.VMEM(pieces, BF16),
            pltpu.VMEM(pieces, BF16),
            pltpu.VMEM((group, rows, tokens), BF16),
            pltpu.VMEM((group, rows, tokens), BF16),
            pltpu.VMEM(queries.shape, BF16),
            pltpu.VMEM(queries.shape, BF16),
            pltpu.VMEM(keyvals.shape, BF16),
            pltpu.VMEM((group, tokens), F32),
            pltpu.SemaphoreType.DMA((3,)),
            pltpu.SemaphoreType.DMA((3,)),
            pltpu.SemaphoreType.DMA(pairs),
            pltpu.SemaphoreType.DMA(pairs),
            pltpu.SemaphoreType.DMA(pairs),
            pltpu.SemaphoreType.DMA(pairs),
        ],
        compiler_params=pltpu.CompilerParams(collective_id=0, has_side_effects=True),
        name="cross_attention",
    )(
        reader_images, read_spans, query_gain.reshape(1, width), key_gain.reshape(1, width),
        keyvals, queries, out_grad,
    )


def solution(mesh):
    placed = (
        P("seq", "tensor"),
        P("seq", "tensor", None),
        P(),
        P(None, "seq"),
        P(),
        P(),
        P("seq", "tensor"),
    )
    return jax.shard_map(
        functools.partial(local, mesh.shape["seq"], mesh.shape["tensor"]),
        mesh=mesh,
        in_specs=placed,
        out_specs=(P("seq", "tensor"), P("seq", "tensor"), P("seq", "tensor", None)),
        check_vma=False,
    )
```

time: 47.8 us -> 24.5 us (0.51)
  Pallas kernels: 0 us -> 19.1 us
  starting transfers between devices: 16.9 us -> 0 us
  waiting for transfers between devices: 14.6 us -> 0 us
  matrix products: 5.42 us -> 0 us
  local copies, waits for them, and re-layouts: 8.1 us -> 4.55 us
  other arithmetic: 1.18 us -> 0 us
    pallas_call x0 -> x1, Pallas kernels: none -> 19.1 us  [local(): pl.pallas_call(functools.partial(kernel, seq_count, tensor_count), out_sh...]
    all_to_all x2 -> x0, starting transfers between devices: 9.63 us -> none  [the longest x1 6.35 us: local(): lax.all_to_all(holder_rows, 'tensor', split_axis=2, concat_axis=1, tiled=...]
    ppermute x4 -> x0, waiting for transfers between devices: 8.43 us -> none  [shifted(): return lax.ppermute(array, axis, pairs)]
    ppermute x4 -> x0, starting transfers between devices: 7.27 us -> none  [shifted(): return lax.ppermute(array, axis, pairs)]
    all_to_all x2 -> x0, waiting for transfers between devices: 6.2 us -> none  [the longest x1 4.01 us: local(): lax.all_to_all(shortened(summed), 'tensor', split_axis=1, concat_axis=2,...]
    dot_general x19 -> x0, matrix products: 5.42 us -> none  [the longest x1 1 us: local(): jnp.dot(selector, at_holder.reshape(slot_total, -1), precision=lax.Precis...]
    reshape x2 -> x0, local copies, waits for them, and re-layouts: 2.14 us -> none  [the longest x1 1.48 us: local(): keyvals.reshape(image_count, sub_rows, tensor_count, 2 * head_width)]
    gather x2 -> x0, local copies, waits for them, and re-layouts: 1.21 us -> none  [the longest x1 0.65 us: local(): picks = reader_images[reader_rows, slot_ids] - my_shard * image_count]
  transfers between devices with their start and end apart: 6 -> 0, of which waited for: 6 -> 0; matrix products, arithmetic and copies ran while one was open for 7% -> 0% of each run, Pallas kernels for 0% -> 0%
where the time goes in v1:
time: 24.5 us; the launch traced here: 24.3 us
  Pallas kernels  19.1 us (78%)
  local copies, waits for them, and re-layouts  4.55 us (19%)
  between operations  0.66 us (3%)
    pallas_call x1, Pallas kernels, local(): pl.pallas_call(functools.partial(kernel, seq_count, tensor_count), out_sh...  19.1 us
    unnamed x10, local copies, waits for them, and re-layouts  4.55 us

profile of v1, /device:TPU:0, one launch (start us, length us, event | category | flops | bytes accessed | tf_op | source)
XLA Modules:
  0.0 24.3 jit_solution(10195395347230473949)
XLA Ops:
  0.6 0.0 copy-start.2
  0.6 0.7 %copy-done.2 = s32[8,3]{0,1:T(4,128)S(1)} copy-done((s32[8,3]{0,1:T(4,128)S(1)}, s32[8,3]{0,1:T(4,128)}, u32[]{:S(2)}) %copy-start.2) | copy-done | bytes 120
  1.3 0.7 %copy.10.images_ref = s32[8,3]{1,0:T(8,128)} copy(s32[8,3]{0,1:T(4,128)S(1)} %copy-done.2) | data formatting | bytes 192 | tf_op args[2]
  2.0 19.1 %cross_attention.1 = (bf16[128,1024]{1,0:T(8,128)(2,1)}, bf16[128,1024]{1,0:T(8,128)(2,1)}, bf16[2,16,1024]{2,1,0:T(8,128)(2,1)}) custom-call(s32[8,3]{1,0:T(8,128)} %copy.10.images_ref, s32[2,128]{1,0:T(2,128)} %spans_ref.1, f32[1,128]{1,0:T(1,128)} %bitcast.2, f32[1,128]{1,0:T(1,128)} %bitcast.3, bf16[2,16,1024]{2,1,0:T(8,128)(2,1)} %kv_hbm.1, ...), custom_call_target="tpu_custom_call" | custom-call | tf_op jit(solution)/shard_map/cross_attention/pallas_call | solution.py:235
  21.1 0.0 copy-start
  21.1 1.7 %copy.14 = bf16[128,1024]{1,0:T(8,128)(2,1)} copy(bf16[128,1024]{1,0:T(8,128)(2,1)} %get-tuple-element.6) | data formatting | bytes 524288
  22.8 0.0 copy-done
  22.8 0.0 copy-start.1
  22.8 0.7 %copy.15 = bf16[128,1024]{1,0:T(8,128)(2,1)} copy(bf16[128,1024]{1,0:T(8,128)(2,1)S(1)} %copy-done) | data formatting | bytes 524288
  23.5 0.2 copy-done.1
  23.6 0.6 %copy.16 = bf16[2,16,1024]{2,1,0:T(8,128)(2,1)} copy(bf16[2,16,1024]{2,1,0:T(8,128)(2,1)S(1)} %copy-done.1) | data formatting | bytes 131072
Async XLA Ops:
  0.6 0.7 %copy-start.2 = (s32[8,3]{0,1:T(4,128)S(1)}, s32[8,3]{0,1:T(4,128)}, u32[]{:S(2)}) copy-start(s32[8,3]{0,1:T(4,128)} %param.9) | copy-start | bytes 292
  21.1 1.7 %copy-start = (bf16[128,1024]{1,0:T(8,128)(2,1)S(1)}, bf16[128,1024]{1,0:T(8,128)(2,1)}, u32[]{:S(2)}) copy-start(bf16[128,1024]{1,0:T(8,128)(2,1)} %get-tuple-element.7) | copy-start | bytes 786436
  22.8 0.9 %copy-start.1 = (bf16[2,16,1024]{2,1,0:T(8,128)(2,1)S(1)}, bf16[2,16,1024]{2,1,0:T(8,128)(2,1)}, u32[]{:S(2)}) copy-start(bf16[2,16,1024]{2,1,0:T(8,128)(2,1)} %get-tuple-element.8) | copy-start | bytes 196612

commit v2 on v1

--- a/solution.py
+++ b/solution.py
@@ -27,9 +27,9 @@
 
 def kernel(
     seq_count, tensor_count,
-    images_ref, spans_ref, query_gain_ref, key_gain_ref, kv_hbm, q_hbm, do_hbm,
+    images_hbm, spans_hbm, query_gain_hbm, key_gain_hbm, kv_hbm, q_hbm, do_hbm,
     att_hbm, qg_hbm, kvg_hbm,
-    kv, q, do, qhat, send, arrive, gsend, garrive, wb, dsb, att, qg, kvg, denoms,
+    images_ref, spans_ref, query_gain_ref, key_gain_ref, kv, q, do, qhat, send, arrive, gsend, garrive, wb, dsb, att, qg, kvg, denoms,
     in_sem, out_sem, send_sem, recv_sem, gsend_sem, grecv_sem,
 ):
     s = lax.axis_index("seq")
@@ -49,7 +49,17 @@
     kv_in = pltpu.make_async_copy(kv_hbm, kv, in_sem.at[0])
     q_in = pltpu.make_async_copy(q_hbm, q, in_sem.at[1])
     do_in = pltpu.make_async_copy(do_hbm, do, in_sem.at[2])
+    small = (
+        (images_hbm, images_ref), (spans_hbm, spans_ref),
+        (query_gain_hbm, query_gain_ref), (key_gain_hbm, key_gain_ref),
+    )
+    small_in = [
+        pltpu.make_async_copy(a, b, in_sem.at[3 + i]) for i, (a, b) in enumerate(small)
+    ]
+    small_in[0].start()
     kv_in.start()
+    for copy in small_in[1:]:
+        copy.start()
     q_in.start()
     do_in.start()
 
@@ -68,10 +78,11 @@
         else:
             pl.when((s + shift >= 0) & (s + shift < seq_count))(greet)
 
+    small_in[0].wait()
     picks = []
     for r in range(slots):
         reader = jnp.minimum(s + r, seq_count - 1)
-        pick = images_ref[reader, r] - s * image_count
+        pick = images_ref[r, reader] - s * image_count
         picks.append(jnp.clip(pick, 0, image_count - 1))
 
     kv_in.wait()
@@ -124,6 +135,8 @@
     for r in reversed(range(slots)):
         each(r, s + r < seq_count, lambda k, r=r: forward(r, k, t).start())
 
+    for copy in small_in[1:]:
+        copy.wait()
     query_gain = query_gain_ref[...]
     key_gain = key_gain_ref[...]
     q_in.wait()
@@ -221,6 +234,15 @@
     kvg_out.wait()
 
 
+def hand_out(att_in, qg_in, kvg_in, att, qg, kvg, sems):
+    pairs = ((att_in, att), (qg_in, qg), (kvg_in, kvg))
+    copies = [pltpu.make_async_copy(a, b, sems.at[i]) for i, (a, b) in enumerate(pairs)]
+    for copy in copies:
+        copy.start()
+    for copy in copies:
+        copy.wait()
+
+
 def local(seq_count, tensor_count, queries, keyvals, reader_images, read_spans, query_gain, key_gain, out_grad):
     width = query_gain.shape[0]
     tokens, columns = queries.shape
@@ -229,19 +251,27 @@
     slots = reader_images.shape[1]
     rows = slots * tensor_count * sub
     pieces = (slots, tensor_count, sub, 2 * width)
-    whole = pl.BlockSpec(memory_space=pltpu.VMEM)
+    held = pl.BlockSpec(memory_space=pltpu.HBM)
     placed = pl.BlockSpec(memory_space=pl.ANY)
     pairs = (slots, tensor_count)
-    return pl.pallas_call(
+    operands = (
+        reader_images.T, read_spans, query_gain.reshape(1, width), key_gain.reshape(1, width),
+        keyvals, queries, out_grad,
+    )
+    results = pl.pallas_call(
         functools.partial(kernel, seq_count, tensor_count),
         out_shape=(
             jax.ShapeDtypeStruct(queries.shape, BF16),
             jax.ShapeDtypeStruct(queries.shape, BF16),
             jax.ShapeDtypeStruct(keyvals.shape, BF16),
         ),
-        in_specs=[pl.BlockSpec(memory_space=pltpu.SMEM), whole, whole, whole, placed, placed, placed],
+        in_specs=[held] * 7,
         out_specs=(placed, placed, placed),
         scratch_shapes=[
+            pltpu.SMEM(reader_images.shape[::-1], jnp.int32),
+            pltpu.VMEM(read_spans.shape, jnp.int32),
+            pltpu.VMEM((1, width), F32),
+            pltpu.VMEM((1, width), F32),
             pltpu.VMEM(keyvals.shape, BF16),
             pltpu.VMEM(queries.shape, BF16),
             pltpu.VMEM(queries.shape, BF16),
@@ -256,19 +286,25 @@
             pltpu.VMEM(queries.shape, BF16),
             pltpu.VMEM(keyvals.shape, BF16),
             pltpu.VMEM((group, tokens), F32),
-            pltpu.SemaphoreType.DMA((3,)),
+            pltpu.SemaphoreType.DMA((7,)),
             pltpu.SemaphoreType.DMA((3,)),
             pltpu.SemaphoreType.DMA(pairs),
             pltpu.SemaphoreType.DMA(pairs),
             pltpu.SemaphoreType.DMA(pairs),
             pltpu.SemaphoreType.DMA(pairs),
         ],
-        compiler_params=pltpu.CompilerParams(collective_id=0, has_side_effects=True),
+        compiler_params=pltpu.CompilerParams(collective_id=0, has_side_effects=True, vmem_limit_bytes=24 * 2**20),
         name="cross_attention",
-    )(
-        reader_images, read_spans, query_gain.reshape(1, width), key_gain.reshape(1, width),
-        keyvals, queries, out_grad,
-    )
+    )(*[pltpu.with_memory_space_constraint(operand, pltpu.HBM) for operand in operands])
+    return pl.pallas_call(
+        hand_out,
+        out_shape=tuple(jax.ShapeDtypeStruct(r.shape, r.dtype) for r in results),
+        in_specs=[placed] * len(results),
+        out_specs=(placed,) * len(results),
+        scratch_shapes=[pltpu.SemaphoreType.DMA((len(results),))],
+        compiler_params=pltpu.CompilerParams(vmem_limit_bytes=2**20),
+        name="hand_out",
+    )(*results)
 
 
 def solution(mesh):

time: 24.5 us -> 19.4 us (0.79)
  local copies, waits for them, and re-layouts: 4.55 us -> 0 us
  Pallas kernels: 19.1 us -> 18.6 us
    unnamed x10 -> x0, local copies, waits for them, and re-layouts: 4.55 us -> none
    pallas_call x1, Pallas kernels: 19.1 us -> 17.8 us  [local(): pl.pallas_call(functools.partial(kernel, seq_count, tensor_count), out_sh...]
    pallas_call x0 -> x1, Pallas kernels: none -> 0.83 us  [local(): pl.pallas_call(hand_out, out_shape=tuple((jax.ShapeDtypeStruct(r.shape, r...]
where the time goes in v2:
time: 19.4 us; the launch traced here: 19.2 us
  Pallas kernels  18.6 us (96%)
  between operations  0.64 us (3%)
    pallas_call x1, Pallas kernels, local(): pl.pallas_call(functools.partial(kernel, seq_count, tensor_count), out_sh...  17.8 us
    pallas_call x1, Pallas kernels, local(): pl.pallas_call(hand_out, out_shape=tuple((jax.ShapeDtypeStruct(r.shape, r...  0.83 us

profile of v2, /device:TPU:0, one launch (start us, length us, event | category | flops | bytes accessed | tf_op | source)
XLA Modules:
  0.0 19.2 jit_solution(6389321666845926022)
XLA Ops:
  0.6 17.8 %cross_attention.1 = (bf16[128,1024]{1,0:T(8,128)(2,1)S(1)}, bf16[128,1024]{1,0:T(8,128)(2,1)S(1)}, bf16[2,16,1024]{2,1,0:T(8,128)(2,1)S(1)}) custom-call(s32[3,8]{1,0:T(4,128)} %bitcast.3, s32[2,128]{1,0:T(2,128)} %spans_hbm.1, f32[1,128]{1,0:T(1,128)} %bitcast.4, f32[1,128]{1,0:T(1,128)} %bitcast.5, bf16[2,16,1024]{2,1,0:T(8,128)(2,1)} %kv_hbm.1, ...), custom_call_target="tpu_custom_call" | custom-call | tf_op jit(solution)/shard_map/cross_attention/pallas_call | solution.py:261
  18.4 0.8 %hand_out.1 = (bf16[128,1024]{1,0:T(8,128)(2,1)}, bf16[128,1024]{1,0:T(8,128)(2,1)}, bf16[2,16,1024]{2,1,0:T(8,128)(2,1)}) custom-call(bf16[128,1024]{1,0:T(8,128)(2,1)S(1)} %get-tuple-element.6.att_in, bf16[128,1024]{1,0:T(8,128)(2,1)S(1)} %get-tuple-element.7.qg_in, bf16[2,16,1024]{2,1,0:T(8,128)(2,1)S(1)} %get-tuple-element.8.kvg_in), custom_call_target="tpu_custom_call" | custom-call | tf_op jit(solution)/shard_map/hand_out/pallas_call | solution.py:299

commit v3 on v2

--- a/solution.py
+++ b/solution.py
@@ -29,7 +29,7 @@
     seq_count, tensor_count,
     images_hbm, spans_hbm, query_gain_hbm, key_gain_hbm, kv_hbm, q_hbm, do_hbm,
     att_hbm, qg_hbm, kvg_hbm,
-    images_ref, spans_ref, query_gain_ref, key_gain_ref, kv, q, do, qhat, send, arrive, gsend, garrive, wb, dsb, att, qg, kvg, denoms,
+    images_ref, spans_ref, query_gain_ref, key_gain_ref, kv, q, do, qhat, send, arrive, gsend, garrive, khat, wf, gp, wb, dsb, att, qg, kvg, denoms,
     in_sem, out_sem, send_sem, recv_sem, gsend_sem, grecv_sem,
 ):
     s = lax.axis_index("seq")
@@ -149,40 +149,46 @@
     ends = spans_ref[1:2, :]
     masks = [((begins <= r) & (r < ends)).astype(F32) for r in range(slots)]
     no_image = 1.0 - functools.reduce(jnp.maximum, masks)
-    mask = jnp.concatenate(
-        [jnp.broadcast_to(m, (image_rows, tokens)) for m in masks], axis=0
-    )
-
+
+    totals = [no_image] * group
+    dots = [jnp.zeros((1, tokens), F32)] * group
     for r in range(slots):
         each(r, s >= r, lambda k, r=r: forward(r, k, from_ring(k)).wait_recv())
-
-    arrived = arrive[...].reshape(all_rows, width2)
-    keys = arrived[:, :width].astype(F32)
-    values = arrived[:, width:]
-    key_hat = (keys * inverse_of(keys) * key_gain).astype(BF16)
-
-    grad_key = jnp.zeros((all_rows, width), F32)
-    grad_value = jnp.zeros((all_rows, width), F32)
+        rows = slice(r * image_rows, (r + 1) * image_rows)
+        keys = arrive[r, :, :, :width].reshape(image_rows, width).astype(F32)
+        value = arrive[r, :, :, width:].reshape(image_rows, width)
+        key_hat = (keys * inverse_of(keys) * key_gain).astype(BF16)
+        khat[rows] = key_hat
+        mask = jnp.broadcast_to(masks[r], (image_rows, tokens))
+        for a in range(group):
+            weights = jnp.exp(dot(key_hat, qhat[a], ROWS) * scale) * mask
+            grad_probs = dot(value, do[:, a * width : (a + 1) * width], ROWS)
+            totals[a] = totals[a] + jnp.sum(weights, axis=0, keepdims=True)
+            dots[a] = dots[a] + jnp.sum(weights * grad_probs, axis=0, keepdims=True)
+            wf[a, rows] = weights
+            gp[a, rows] = grad_probs
+            wb[a, rows] = weights.astype(BF16)
+
     for a in range(group):
-        grad_out = do[:, a * width : (a + 1) * width]
-        query = qhat[a]
-        weights = jnp.exp(dot(key_hat, query, ROWS) * scale) * mask
-        denominator = jnp.sum(weights, axis=0, keepdims=True) + no_image
-        probs = weights * (1.0 / denominator)
-        grad_probs = dot(values, grad_out, ROWS)
-        row_dot = jnp.sum(probs * grad_probs, axis=0, keepdims=True)
-        score_grad = (probs * (grad_probs - row_dot)).astype(BF16)
-        wb[a] = weights.astype(BF16)
-        dsb[a] = score_grad
-        denoms[a : a + 1, :] = denominator
-        grad_key = grad_key + dot(score_grad, query)
-        grad_value = grad_value + dot(probs.astype(BF16), grad_out)
-    piece = (slots, tensor_count, sub, width)
-    gsend[:, :, :, :width] = (grad_key * scale).astype(BF16).reshape(piece)
-    gsend[:, :, :, width:] = grad_value.astype(BF16).reshape(piece)
-
+        denoms[a : a + 1, :] = totals[a]
+    inverses = [1.0 / total for total in totals]
+    row_dots = [d * i for d, i in zip(dots, inverses)]
     for r in reversed(range(slots)):
+        rows = slice(r * image_rows, (r + 1) * image_rows)
+        grad_key = jnp.zeros((image_rows, width), F32)
+        grad_value = jnp.zeros((image_rows, width), F32)
+        for a in range(group):
+            probs = wf[a, rows] * inverses[a]
+            score_grad = (probs * (gp[a, rows] - row_dots[a])).astype(BF16)
+            dsb[a, rows] = score_grad
+            grad_key = grad_key + dot(score_grad, qhat[a])
+            grad_value = grad_value + dot(probs.astype(BF16), do[:, a * width : (a + 1) * width])
+        piece = (tensor_count, sub, width)
+        gsend[r, :, :, :width] = (grad_key * scale).astype(BF16).reshape(piece)
+        gsend[r, :, :, width:] = grad_value.astype(BF16).reshape(piece)
         each(r, s >= r, lambda k, r=r: backward(r, k, t).start())
+    key_hat = khat[...]
+    values = arrive[:, :, :, width:].reshape(all_rows, width)
     garrive[0, t] = gsend[0, t]
 
     padded = jnp.concatenate(
@@ -280,6 +286,9 @@
             pltpu.VMEM(pieces, BF16),
             pltpu.VMEM(pieces, BF16),
             pltpu.VMEM(pieces, BF16),
+            pltpu.VMEM((rows, width), BF16),
+            pltpu.VMEM((group, rows, tokens), F32),
+            pltpu.VMEM((group, rows, tokens), F32),
             pltpu.VMEM((group, rows, tokens), BF16),
             pltpu.VMEM((group, rows, tokens), BF16),
             pltpu.VMEM(queries.shape, BF16),

time: 19.4 us -> 19 us (0.979)
  Pallas kernels: 18.6 us -> 18.2 us
    pallas_call x1, Pallas kernels: 17.8 us -> 17.3 us  [local(): pl.pallas_call(functools.partial(kernel, seq_count, tensor_count), out_sh...]
where the time goes in v3:
time: 19 us; the launch traced here: 18.8 us
  Pallas kernels  18.2 us (96%)
  between operations  0.64 us (3%)
    pallas_call x1, Pallas kernels, local(): pl.pallas_call(functools.partial(kernel, seq_count, tensor_count), out_sh...  17.3 us
    pallas_call x1, Pallas kernels, local(): pl.pallas_call(hand_out, out_shape=tuple((jax.ShapeDtypeStruct(r.shape, r...  0.83 us

profile of v3, /device:TPU:0, one launch (start us, length us, event | category | flops | bytes accessed | tf_op | source)
XLA Modules:
  0.0 18.8 jit_solution(9350727686960946689)
XLA Ops:
  0.6 17.3 %cross_attention.1 = (bf16[128,1024]{1,0:T(8,128)(2,1)S(1)}, bf16[128,1024]{1,0:T(8,128)(2,1)S(1)}, bf16[2,16,1024]{2,1,0:T(8,128)(2,1)S(1)}) custom-call(s32[3,8]{1,0:T(4,128)} %bitcast.3, s32[2,128]{1,0:T(2,128)} %spans_hbm.1, f32[1,128]{1,0:T(1,128)} %bitcast.4, f32[1,128]{1,0:T(1,128)} %bitcast.5, bf16[2,16,1024]{2,1,0:T(8,128)(2,1)} %kv_hbm.1, ...), custom_call_target="tpu_custom_call" | custom-call | tf_op jit(solution)/shard_map/cross_attention/pallas_call | solution.py:267
  18.0 0.8 %hand_out.1 = (bf16[128,1024]{1,0:T(8,128)(2,1)}, bf16[128,1024]{1,0:T(8,128)(2,1)}, bf16[2,16,1024]{2,1,0:T(8,128)(2,1)}) custom-call(bf16[128,1024]{1,0:T(8,128)(2,1)S(1)} %get-tuple-element.6.att_in, bf16[128,1024]{1,0:T(8,128)(2,1)S(1)} %get-tuple-element.7.qg_in, bf16[2,16,1024]{2,1,0:T(8,128)(2,1)S(1)} %get-tuple-element.8.kvg_in), custom_call_target="tpu_custom_call" | custom-call | tf_op jit(solution)/shard_map/hand_out/pallas_call | solution.py:308

commit v4 on v3

--- a/solution.py
+++ b/solution.py
@@ -29,7 +29,7 @@
     seq_count, tensor_count,
     images_hbm, spans_hbm, query_gain_hbm, key_gain_hbm, kv_hbm, q_hbm, do_hbm,
     att_hbm, qg_hbm, kvg_hbm,
-    images_ref, spans_ref, query_gain_ref, key_gain_ref, kv, q, do, qhat, send, arrive, gsend, garrive, khat, wf, gp, wb, dsb, att, qg, kvg, denoms,
+    images_ref, spans_ref, query_gain_ref, key_gain_ref, kv, q, do, qhat, send, arrive, gsend, garrive, khat, wf, gp, wb, dsb, att, qg, kvg, denoms, gains, cubes, products, sums,
     in_sem, out_sem, send_sem, recv_sem, gsend_sem, grecv_sem,
 ):
     s = lax.axis_index("seq")
@@ -211,40 +211,65 @@
     qg_out = pltpu.make_async_copy(qg, qg_hbm, out_sem.at[1])
     qg_out.start()
 
-    for r in range(slots):
-        each(r, s + r < seq_count, lambda k, r=r: backward(r, k, from_ring(k)).wait_recv())
-
     for i in range(image_count):
-        chosen = [(picks[r] == i) & (s + r < seq_count) for r in range(slots)]
         for h in range(tensor_count):
-            total = jnp.zeros((sub, width2), F32)
-            for r in range(slots):
-                total = total + jnp.where(chosen[r], garrive[r, h].astype(F32), 0.0)
             start = h * width2
             raw = kv[i, :, start : start + width].astype(F32)
             inverse = inverse_of(raw)
-            scaled = key_gain * total[:, :width]
-            mean = jnp.mean(raw * scaled, axis=-1, keepdims=True)
+            gains[i, h] = key_gain * inverse
+            cubes[i, h] = raw * (inverse * inverse * inverse)
+            products[i, h] = raw * key_gain
+
+    chosen = [
+        [(picks[r] == i) & (s + r < seq_count) for r in range(slots)]
+        for i in range(image_count)
+    ]
+
+    def taken(i, h, r):
+        return jnp.where(chosen[i][r], garrive[r, h].astype(F32), 0.0)
+
+    for r in range(slots):
+        each(r, s + r < seq_count, lambda k, r=r: backward(r, k, from_ring(k)).wait_recv())
+        if r + 1 == slots:
+            break
+        for i in range(image_count):
+            for h in range(tensor_count):
+                sums[i, h] = taken(i, h, r) + (sums[i, h] if r else 0.0)
+
+    kvg_out = []
+    for i in range(image_count):
+        for h in range(tensor_count):
+            total = taken(i, h, slots - 1) + (sums[i, h] if slots > 1 else 0.0)
+            start = h * width2
+            grad = total[:, :width]
+            mean = jnp.mean(products[i, h] * grad, axis=-1, keepdims=True)
             kvg[i, :, start : start + width] = (
-                inverse * scaled - raw * (inverse * inverse * inverse * mean)
+                gains[i, h] * grad - cubes[i, h] * mean
             ).astype(BF16)
             kvg[i, :, start + width : start + width2] = total[:, width:].astype(BF16)
-    kvg_out = pltpu.make_async_copy(kvg, kvg_hbm, out_sem.at[2])
-    kvg_out.start()
+        kvg_out.append(pltpu.make_async_copy(kvg.at[i], kvg_hbm.at[i], out_sem.at[2 + i]))
+        kvg_out[i].start()
 
     for r in range(slots):
         each(r, s + r < seq_count, lambda k, r=r: forward(r, k, t).wait_send())
         each(r, s >= r, lambda k, r=r: backward(r, k, t).wait_send())
     att_out.wait()
     qg_out.wait()
-    kvg_out.wait()
+    for copy in kvg_out:
+        copy.wait()
 
 
 def hand_out(att_in, qg_in, kvg_in, att, qg, kvg, sems):
-    pairs = ((att_in, att), (qg_in, qg), (kvg_in, kvg))
-    copies = [pltpu.make_async_copy(a, b, sems.at[i]) for i, (a, b) in enumerate(pairs)]
-    for copy in copies:
-        copy.start()
+    copies = []
+    for source, target in ((att_in, att), (qg_in, qg), (kvg_in, kvg)):
+        count = source.shape[0]
+        cuts = min(sems.shape[1], count)
+        size = -(-count // cuts)
+        for start in range(0, count, size):
+            part = pl.ds(start, min(size, count - start))
+            sem = sems.at[len(copies) // sems.shape[1], len(copies) % sems.shape[1]]
+            copies.append(pltpu.make_async_copy(source.at[part], target.at[part], sem))
+            copies[-1].start()
     for copy in copies:
         copy.wait()
 
@@ -295,8 +320,12 @@
             pltpu.VMEM(queries.shape, BF16),
             pltpu.VMEM(keyvals.shape, BF16),
             pltpu.VMEM((group, tokens), F32),
+            pltpu.VMEM((image_count, tensor_count, sub, width), F32),
+            pltpu.VMEM((image_count, tensor_count, sub, width), F32),
+            pltpu.VMEM((image_count, tensor_count, sub, width), F32),
+            pltpu.VMEM((image_count, tensor_count, sub, 2 * width), F32),
             pltpu.SemaphoreType.DMA((7,)),
-            pltpu.SemaphoreType.DMA((3,)),
+            pltpu.SemaphoreType.DMA((2 + image_count,)),
             pltpu.SemaphoreType.DMA(pairs),
             pltpu.SemaphoreType.DMA(pairs),
             pltpu.SemaphoreType.DMA(pairs),
@@ -310,7 +339,7 @@
         out_shape=tuple(jax.ShapeDtypeStruct(r.shape, r.dtype) for r in results),
         in_specs=[placed] * len(results),
         out_specs=(placed,) * len(results),
-        scratch_shapes=[pltpu.SemaphoreType.DMA((len(results),))],
+        scratch_shapes=[pltpu.SemaphoreType.DMA((len(results), 4))],
         compiler_params=pltpu.CompilerParams(vmem_limit_bytes=2**20),
         name="hand_out",
     )(*results)

time: 19 us -> 19.1 us (level)
  no operation moved by 1% of the time
where the time goes in v4:
time: 19.1 us; the launch traced here: 18.9 us
  Pallas kernels  18.3 us (96%)
  between operations  0.64 us (3%)
    pallas_call x1, Pallas kernels, local(): pl.pallas_call(functools.partial(kernel, seq_count, tensor_count), out_sh...  17.4 us
    pallas_call x1, Pallas kernels, local(): pl.pallas_call(hand_out, out_shape=tuple((jax.ShapeDtypeStruct(r.shape, r...  0.9 us

profile of v4, /device:TPU:0, one launch (start us, length us, event | category | flops | bytes accessed | tf_op | source)
XLA Modules:
  0.0 18.9 jit_solution(3055464042181659872)
XLA Ops:
  0.6 17.4 %cross_attention.1 = (bf16[128,1024]{1,0:T(8,128)(2,1)S(1)}, bf16[128,1024]{1,0:T(8,128)(2,1)S(1)}, bf16[2,16,1024]{2,1,0:T(8,128)(2,1)S(1)}) custom-call(s32[3,8]{1,0:T(4,128)} %bitcast.3, s32[2,128]{1,0:T(2,128)} %spans_hbm.1, f32[1,128]{1,0:T(1,128)} %bitcast.4, f32[1,128]{1,0:T(1,128)} %bitcast.5, bf16[2,16,1024]{2,1,0:T(8,128)(2,1)} %kv_hbm.1, ...), custom_call_target="tpu_custom_call" | custom-call | tf_op jit(solution)/shard_map/cross_attention/pallas_call | solution.py:292
  18.0 0.9 %hand_out.1 = (bf16[128,1024]{1,0:T(8,128)(2,1)}, bf16[128,1024]{1,0:T(8,128)(2,1)}, bf16[2,16,1024]{2,1,0:T(8,128)(2,1)}) custom-call(bf16[128,1024]{1,0:T(8,128)(2,1)S(1)} %get-tuple-element.6.att_in, bf16[128,1024]{1,0:T(8,128)(2,1)S(1)} %get-tuple-element.7.qg_in, bf16[2,16,1024]{2,1,0:T(8,128)(2,1)S(1)} %get-tuple-element.8.kvg_in), custom_call_target="tpu_custom_call" | custom-call | tf_op jit(solution)/shard_map/hand_out/pallas_call | solution.py:337

commit v5 on v4

--- a/solution.py
+++ b/solution.py
@@ -152,7 +152,7 @@
 
     totals = [no_image] * group
     dots = [jnp.zeros((1, tokens), F32)] * group
-    for r in range(slots):
+    for r in (0, *range(slots - 1, 0, -1)):
         each(r, s >= r, lambda k, r=r: forward(r, k, from_ring(k)).wait_recv())
         rows = slice(r * image_rows, (r + 1) * image_rows)
         keys = arrive[r, :, :, :width].reshape(image_rows, width).astype(F32)
@@ -339,7 +339,7 @@
         out_shape=tuple(jax.ShapeDtypeStruct(r.shape, r.dtype) for r in results),
         in_specs=[placed] * len(results),
         out_specs=(placed,) * len(results),
-        scratch_shapes=[pltpu.SemaphoreType.DMA((len(results), 4))],
+        scratch_shapes=[pltpu.SemaphoreType.DMA((len(results), 1))],
         compiler_params=pltpu.CompilerParams(vmem_limit_bytes=2**20),
         name="hand_out",
     )(*results)

time: 19.1 us -> 19 us (level)
  no operation moved by 1% of the time
where the time goes in v5:
time: 19 us; the launch traced here: 18.8 us
  Pallas kernels  18.2 us (96%)
  between operations  0.64 us (3%)
    pallas_call x1, Pallas kernels, local(): pl.pallas_call(functools.partial(kernel, seq_count, tensor_count), out_sh...  17.4 us
    pallas_call x1, Pallas kernels, local(): pl.pallas_call(hand_out, out_shape=tuple((jax.ShapeDtypeStruct(r.shape, r...  0.83 us

profile of v5, /device:TPU:0, one launch (start us, length us, event | category | flops | bytes accessed | tf_op | source)
XLA Modules:
  0.0 18.8 jit_solution(9405881811007655322)
XLA Ops:
  0.6 17.4 %cross_attention.1 = (bf16[128,1024]{1,0:T(8,128)(2,1)S(1)}, bf16[128,1024]{1,0:T(8,128)(2,1)S(1)}, bf16[2,16,1024]{2,1,0:T(8,128)(2,1)S(1)}) custom-call(s32[3,8]{1,0:T(4,128)} %bitcast.3, s32[2,128]{1,0:T(2,128)} %spans_hbm.1, f32[1,128]{1,0:T(1,128)} %bitcast.4, f32[1,128]{1,0:T(1,128)} %bitcast.5, bf16[2,16,1024]{2,1,0:T(8,128)(2,1)} %kv_hbm.1, ...), custom_call_target="tpu_custom_call" | custom-call | tf_op jit(solution)/shard_map/cross_attention/pallas_call | solution.py:292
  18.0 0.8 %hand_out.1 = (bf16[128,1024]{1,0:T(8,128)(2,1)}, bf16[128,1024]{1,0:T(8,128)(2,1)}, bf16[2,16,1024]{2,1,0:T(8,128)(2,1)}) custom-call(bf16[128,1024]{1,0:T(8,128)(2,1)S(1)} %get-tuple-element.6.att_in, bf16[128,1024]{1,0:T(8,128)(2,1)S(1)} %get-tuple-element.7.qg_in, bf16[2,16,1024]{2,1,0:T(8,128)(2,1)S(1)} %get-tuple-element.8.kvg_in), custom_call_target="tpu_custom_call" | custom-call | tf_op jit(solution)/shard_map/hand_out/pallas_call | solution.py:337
